TPU v7x, 32 devices: a whole 2x2x4 slice. The times are simulated.
32 devices in a mesh: ctx: 8 (over z, y), grp: 2 (over core), head: 2 (over x).
Axes of the slice: x: 2, y: 2, z: 4, core: 2. Of those that a mesh axis runs over, the one named last changes fastest.
Arguments:
- residual: bfloat16 [2048, 2880], P(('ctx', 'grp')), may hold values from -10 to 10
- queries: bfloat16 [2048, 2048], P(('ctx', 'grp'), 'head'), may hold values from -32 to 32
- keys: bfloat16 [2048, 256], P(('ctx', 'grp'), 'head'), may hold values from -32 to 32
- values: bfloat16 [2048, 256], P(('ctx', 'grp'), 'head'), may hold values from -12 to 12
- out_weight: bfloat16 [2048, 2880], P('head'), may hold values from -0.125 to 0.125
- norm_gain: float32 [2880], replicated, may hold values from 0.5 to 1.5
- routes: int32 [2048, 4], P(('ctx', 'grp')), may hold values from 0 to 7, all different within a row; in each aligned block of 128 rows (0 to 127, 128 to 255, ...) at most 72 rows name the same one
- expert_weight: bfloat16 [8, 2880, 2, 1536], P('ctx', None, None, 'head'), may hold values from -0.109375 to 0.109375
Outputs:
- hidden: bfloat16 [2048, 2880], P(('ctx', 'grp'), 'head')
- active: bfloat16 [8, 2, 576, 1536], P('ctx', 'grp', None, 'head')
Inputs may be any that keep to these rules, and one draw needn't show every extreme that they name: `routes`: each token names 4 different experts; the 128 rows of one device name any one expert at most 72 times.
All inputs are finite; a program needn't handle non-finite values.
Results may differ from a plain program's by a relative error of at most 0.017.
Values may be sent and summed in bfloat16 or wider, within the bound.
A program may use at most 128 MiB of HBM per device.

v0:
```python
import jax
import jax.numpy as jnp
from jax import lax
from jax.sharding import PartitionSpec as P

D = 2880
HD = 64
TOP = 4


def shifted(value, axis, by):
    count = lax.axis_size(axis)
    pairs = [(i, i + by) for i in range(count) if 0 <= i + by < count]
    return lax.ppermute(value, axis, pairs)


def attend_block(running, query_heads, key_block, value_block, query_place, key_place, band):
    allowed = (
        (key_place[None, :] <= query_place[:, None])
        & (query_place[:, None] - key_place[None, :] < band)
        & (key_place[None, :] >= 0)
    )

    def attend_live(carried):
        row_max, row_total, summed = carried
        scores = jnp.einsum(
            "tkgd,skd->kgts", query_heads, key_block, preferred_element_type=jnp.float32
        )
        scores = jnp.where(allowed, scores * query_heads.shape[-1] ** (-0.5), -1e30)
        new_max = jnp.maximum(row_max, jnp.max(scores, axis=-1))
        weights = jnp.where(allowed, jnp.exp(scores - new_max[..., None]), 0.0)
        factor = jnp.exp(row_max - new_max)
        row_total = row_total * factor + jnp.sum(weights, axis=-1)
        summed = summed * factor[..., None] + jnp.einsum(
            "kgts,skd->kgtd",
            weights.astype(jnp.bfloat16),
            value_block,
            preferred_element_type=jnp.float32,
        )
        return (new_max, row_total, summed)

    def skip_block(carried):
        return carried

    return lax.cond(jnp.any(allowed), attend_live, skip_block, running)


def finish_rows(gate_up, squares, hidden_width):
    inverse_rms = lax.rsqrt(squares / D + 1e-05)
    gate_part = gate_up[..., :hidden_width] * inverse_rms[..., None]
    up_part = gate_up[..., hidden_width:] * inverse_rms[..., None]
    return (gate_part * jax.nn.sigmoid(1.702 * gate_part) * (up_part + 1.0)).astype(jnp.bfloat16)


def body(residual, queries, keys, values, out_weight, norm_gain, routes, expert_weight):
    tokens_here = queries.shape[0]
    kv_local = keys.shape[1] // HD
    per_group = queries.shape[1] // keys.shape[1]
    query_heads = queries.reshape(tokens_here, kv_local, per_group, HD)
    ctx_index = lax.axis_index("ctx")
    grp_index = lax.axis_index("grp")
    head_index = lax.axis_index("head")
    heads_count = lax.axis_size("head")
    block_len = tokens_here * lax.axis_size("grp")
    reach_steps = max(1, lax.axis_size("ctx") // 16)
    band = reach_steps * block_len
    query_place = (
        ctx_index * block_len + grp_index * tokens_here + jnp.arange(tokens_here, dtype=jnp.int32)
    )
    own_keys, own_values = (
        lax.all_gather(keys, "grp", axis=0, tiled=True),
        lax.all_gather(values, "grp", axis=0, tiled=True),
    )

    def attend_from(running, key_flat, value_flat, distance):
        key_place = (ctx_index - distance) * block_len + jnp.arange(block_len, dtype=jnp.int32)
        return attend_block(
            running,
            query_heads,
            key_flat.reshape(block_len, kv_local, HD),
            value_flat.reshape(block_len, kv_local, HD),
            query_place,
            key_place,
            band,
        )

    running = (
        jnp.full((kv_local, per_group, tokens_here), -1e30, jnp.float32),
        jnp.zeros((kv_local, per_group, tokens_here), jnp.float32),
        jnp.zeros((kv_local, per_group, tokens_here, HD), jnp.float32),
    )
    running = attend_from(running, own_keys, own_values, 0)

    def cycle_turn(distance, carried):
        running, key_flat, value_flat = carried
        key_flat, value_flat = shifted((key_flat, value_flat), "ctx", 1)
        running = attend_from(running, key_flat, value_flat, distance)
        return (running, key_flat, value_flat)

    running = lax.fori_loop(1, reach_steps + 1, cycle_turn, (running, own_keys, own_values))[0]
    row_max, row_total, summed = running
    mixed = summed / row_total[..., None]
    attended = (
        jnp.transpose(mixed, (2, 0, 1, 3))
        .reshape(tokens_here, kv_local * per_group * HD)
        .astype(jnp.bfloat16)
    )
    partial_value = jnp.dot(attended, out_weight, preferred_element_type=jnp.float32)
    column_width = D // heads_count
    experts_all = expert_weight.shape[0] * lax.axis_size("ctx")
    routed = tokens_here * TOP
    capacity = min(tokens_here, routed // experts_all + max(1, routed // (8 * experts_all)))
    flat_routes = routes.reshape(routed)
    expert_hits = (
        flat_routes[:, None] == jnp.arange(experts_all, dtype=jnp.int32)[None, :]
    ).astype(jnp.bfloat16)
    earlier = jnp.tril(jnp.ones((routed, routed), jnp.bfloat16), -1)
    before = jnp.dot(earlier, expert_hits, preferred_element_type=jnp.float32)
    slot_index = jnp.sum(before * expert_hits.astype(jnp.float32), axis=1).astype(jnp.int32)
    hidden_width = expert_weight.shape[3]
    local_weight = expert_weight[0].reshape(D, 2 * hidden_width)
    projected = lax.psum_scatter(
        partial_value.astype(jnp.bfloat16), "head", scatter_dimension=1, tiled=True
    ).astype(jnp.float32)
    own_residual = lax.dynamic_slice_in_dim(residual, head_index * column_width, column_width, 1)
    hidden = (own_residual.astype(jnp.float32) + projected).astype(jnp.bfloat16)
    dest_index = flat_routes * capacity + slot_index
    route_rows = jnp.repeat(hidden, TOP, axis=0)
    outgoing = (
        jnp.zeros((experts_all * capacity, column_width), jnp.bfloat16)
        .at[dest_index]
        .set(route_rows)
    )
    arrived = lax.all_to_all(
        outgoing.reshape(experts_all, capacity, column_width),
        "ctx",
        split_axis=0,
        concat_axis=1,
        tiled=True,
    )
    arrived_rows = arrived.reshape(-1, column_width)
    slot_total = arrived_rows.shape[0]
    widened = lax.all_gather(arrived_rows, "head", axis=1, tiled=True).astype(jnp.float32)
    scaled = (widened * norm_gain[None, :]).astype(jnp.bfloat16)
    gate_up = jnp.dot(scaled, local_weight, preferred_element_type=jnp.float32)
    squares = jnp.sum(widened * widened, axis=1)
    gate_up, squares = (gate_up, squares)
    active = finish_rows(gate_up, squares, hidden_width)
    return (hidden, active.reshape(1, 1, slot_total, hidden_width))


def solution(mesh):
    in_specs = (
        P(("ctx", "grp"), None),
        P(("ctx", "grp"), "head"),
        P(("ctx", "grp"), "head"),
        P(("ctx", "grp"), "head"),
        P("head", None),
        P(),
        P(("ctx", "grp"), None),
        P("ctx", None, None, "head"),
    )
    out_specs = (P(("ctx", "grp"), "head"), P("ctx", "grp", None, "head"))
    return jax.shard_map(body, mesh=mesh, in_specs=in_specs, out_specs=out_specs, check_vma=False)
```

profile of v0, /device:TPU:0, one launch (start us, length us, event | category | flops | bytes accessed | tf_op | source)
XLA Modules:
  0.0 196.8 jit_solution(11392658521346276499)
XLA Ops:
  7.2 0.0 reduce-scatter.2.cloned.1.call-start
  7.2 0.9 copy.35
  8.1 2.2 %all_gather.9 = bf16[256,128]{0,1:T(8,128)(2,1)} all-gather(bf16[128,128]{0,1:T(8,128)(2,1)S(1)} %copy.35), channel_id=1, replica_groups=mesh['ctx'=8,'grp'=2,'head'=2] {'grp'}, dimensions={0}, use_global_device_ids=true | all-gather | bytes 98304 | tf_op jit(solution)/shard_map/all_gather | solution.py:71
  10.2 4.7 %collective-permute-start = (bf16[256,128]{0,1:T(8,128)(2,1)}, bf16[256,128]{0,1:T(8,128)(2,1)S(1)}, u32[]{:S(2)}, u32[]{:S(2)}) collective-permute-start(bf16[256,128]{0,1:T(8,128)(2,1)} %all_gather.9), channel_id=1, source_target_pairs={{0,4},{4,8},{8,12},{12,16},{16,20},{20,24},{24,28},{1,5},{5,9},{9,... | collective-permute-start | bytes 196616 | tf_op jit(solution)/shard_map/while/body/eval_jaxpr/ppermute | solution.py:14
  15.0 0.9 copy.37
  15.9 2.0 %all_gather.10 = bf16[256,128]{0,1:T(8,128)(2,1)} all-gather(bf16[128,128]{0,1:T(8,128)(2,1)S(1)} %copy.37), channel_id=1, replica_groups=mesh['ctx'=8,'grp'=2,'head'=2] {'grp'}, dimensions={0}, use_global_device_ids=true | all-gather | bytes 98304 | tf_op jit(solution)/shard_map/all_gather | solution.py:72
  17.9 3.4 %collective-permute-start.1 = (bf16[256,128]{0,1:T(8,128)(2,1)}, bf16[256,128]{0,1:T(8,128)(2,1)S(1)}, u32[]{:S(2)}, u32[]{:S(2)}) collective-permute-start(bf16[256,128]{0,1:T(8,128)(2,1)} %all_gather.10), channel_id=1, source_target_pairs={{0,4},{4,8},{8,12},{12,16},{16,20},{20,24},{24,28},{1,5},{5,9},{9,... | collective-permute-start | bytes 196616 | tf_op jit(solution)/shard_map/while/body/eval_jaxpr/ppermute | solution.py:14
  21.4 0.8 fusion.45
  22.2 1.1 copy.36
  24.6 5.3 %conditional.2 = (f32[2,8,128]{2,1,0:T(8,128)}, f32[2,8,128]{2,1,0:T(8,128)S(1)}, f32[2,8,128,64]{2,3,1,0:T(8,128)S(1)}) conditional(s32[]{:T(128)} %convert_element_type.65, () %tuple.30, (pred[128,256]{0,1:T(8,128)(4,1)S(1)}, bf16[256,128]{0,1:T(8,128)(2,1)}, bf16[128,2,8,64]{0,3,2,1:T(8,128)(2,1)S(1)}, bf16[256,128]{0,1:T(8,128)(2,1)}) %tuple.54), branch_computations={%region_2.3_spmd, %region_3.6_spmd} | conditional | flops 141172736 | bytes 7397400 | solution.py:45
  24.6 1.3 fusion
  26.0 0.6 exponential_multiply_fusion
  26.6 1.4 convolution_add_fusion
  28.0 1.2 fusion.2
  29.2 0.7 fusion.11
  29.9 0.0 collective-permute-done
  29.9 0.0 collective-permute-done.1
  30.0 0.1 divide_convert_fusion
  30.0 0.0 copy-start.3
  30.0 5.2 %convolution_convert_fusion = bf16[128,2880]{0,1:T(8,128)(2,1)} fusion(bf16[1024,2880]{0,1:T(8,128)(2,1)} %param.16, bf16[128,1024]{0,1:T(8,128)(2,1)S(1)} %bitcast.76), kind=kOutput, calls=%fused_computation.34 | convolution fusion | flops 755343360 | bytes 6897664 | tf_op jit(solution)/shard_map/dot_general | solution.py:108
  35.3 0.0 copy-start.2
  35.3 0.0 reduce-scatter.2.cloned.1.call-update
  35.3 0.0 all-gather.3.cloned.1.call-start
  35.4 0.0 copy-done.3
  35.4 0.1 copy.39
  35.5 0.1 eq.15
  35.6 0.3 fusion.28
  36.0 0.1 copy.38
  36.1 0.1 mul.108
  36.2 19.5 %reduce-scatter.2.cloned.1.call-done = bf16[128,1440]{0,1:T(8,128)(2,1)} async-done(((bf16[128,2880]{0,1:T(8,128)(2,1)}), bf16[128,1440]{0,1:T(8,128)(2,1)}) %reduce-scatter.2.cloned.1.call-update) | async-done | bytes 368656 | tf_op jit(solution)/shard_map/reduce_scatter | solution.py:122
  55.7 0.0 copy-done.2
  55.7 1.1 add_convert_fusion
  56.8 0.0 copy-start.1
  56.8 0.7 copy-done.1
  57.6 0.2 copy.40
  57.8 0.4 broadcast_in_dim.79
  58.2 0.8 reshape.122
  59.0 3.5 %scatter_custom_fusion = bf16[576,1440]{1,0:T(8,128)(2,1)S(1)} fusion(s32[512]{0:T(512)S(1)} %bitcast.79, bf16[512,1440]{1,0:T(8,128)(2,1)S(1)} %reshape.122, bf16[]{:T(256)} %constant.49.clone.1), kind=kCustom, calls=%fused_computation.46 | custom fusion | bytes 1658882 | tf_op jit(solution)/shard_map/scatter | solution.py:132
  62.5 46.6 %all_to_all.4 = bf16[8,72,1440]{2,1,0:T(8,128)(2,1)} all-to-all(bf16[8,72,1440]{2,1,0:T(8,128)(2,1)S(1)} %bitcast.73), channel_id=1, replica_groups=mesh['ctx'=8,'grp'=2,'head'=2] {'ctx'}, dimensions={0} | all-to-all | bytes 3317760 | tf_op jit(solution)/shard_map/all_to_all | solution.py:134
  109.1 0.0 all-gather.3.cloned.1.call-update
  109.1 9.0 %copy.48 = bf16[360,8,2,768]{3,1,2,0:T(8,128)(2,1)} copy(bf16[360,8,2,768]{3,2,1,0:T(2,128)(2,1)} %bitcast.70) | data formatting | bytes 17694720
  118.1 38.5 %all-gather.3.cloned.1.call-done = bf16[2,1440,576]{1,2,0:T(8,128)(2,1)} async-done(((bf16[1,1440,576]{1,2,0:T(8,128)(2,1)}), bf16[2,1440,576]{1,2,0:T(8,128)(2,1)}) %all-gather.3.cloned.1.call-update) | async-done | bytes 3317776 | tf_op jit(solution)/shard_map/all_gather | solution.py:143
  156.5 8.6 %copy.41 = f32[2,1440,576]{1,0,2:T(2,128)} copy(bf16[2,1440,576]{1,2,0:T(8,128)(2,1)} %all-gather.3.cloned.1.call-done) | data formatting | bytes 9953280 | tf_op jit(solution)/shard_map/convert_element_type | solution.py:143
  165.1 10.2 %reshape.128 = f32[2880,576]{0,1:T(8,128)} reshape(f32[2,1440,576]{1,0,2:T(2,128)} %copy.41) | data formatting | bytes 13271040 | tf_op jit(solution)/shard_map/convert_element_type | solution.py:143
  175.3 0.0 copy-start
  175.3 0.0 copy-start.4
  175.3 3.6 %multiply_reduce_fusion = f32[576]{0:T(1024)S(1)} fusion(f32[2880,576]{0,1:T(8,128)} %reshape.128), kind=kLoop, calls=%fused_computation.32 | loop fusion | flops 3317184 | bytes 6637824 | tf_op jit(solution)/shard_map/reduce_sum | solution.py:146
  178.9 1.2 copy-done
  180.2 0.0 copy-done.4
  180.2 8.2 %fusion.23 = f32[576,1536]{1,0:T(8,128)S(1)} fusion(bf16[2880,1536]{1,0:T(8,128)(2,1)} %bitcast.71, f32[2880,576]{0,1:T(8,128)S(1)} %copy-done, f32[2880]{0:T(1024)S(1)} %copy-done.4), kind=kOutput, calls=%fused_computation.35 | convolution fusion | flops 5099397120 | bytes 19033344 | tf_op jit(solution)/shard_map/dot_general | solution.py:145
  188.4 1.6 fusion.32
  (9 shorter events, 0.1 us)
Async XLA Ops:
  7.2 48.6 %reduce-scatter.2.cloned.1.call-start = ((), (), s32[]{:S(2)}) async-start(), calls=%async_computation.2 | async-start | bytes 1105920 | tf_op jit(solution)/shard_map/reduce_scatter | solution.py:122
  10.2 19.7 %collective-permute-start = (bf16[256,128]{0,1:T(8,128)(2,1)}, bf16[256,128]{0,1:T(8,128)(2,1)S(1)}, u32[]{:S(2)}, u32[]{:S(2)}) collective-permute-start(bf16[256,128]{0,1:T(8,128)(2,1)} %all_gather.9), channel_id=1, source_target_pairs={{0,4},{4,8},{8,12},{12,16},{16,20},{20,24},{24,28},{1,5},{5,9},{9,... | collective-permute-start | bytes 196616 | tf_op jit(solution)/shard_map/while/body/eval_jaxpr/ppermute | solution.py:14
  17.9 12.1 %collective-permute-start.1 = (bf16[256,128]{0,1:T(8,128)(2,1)}, bf16[256,128]{0,1:T(8,128)(2,1)S(1)}, u32[]{:S(2)}, u32[]{:S(2)}) collective-permute-start(bf16[256,128]{0,1:T(8,128)(2,1)} %all_gather.10), channel_id=1, source_target_pairs={{0,4},{4,8},{8,12},{12,16},{16,20},{20,24},{24,28},{1,5},{5,9},{9,... | collective-permute-start | bytes 196616 | tf_op jit(solution)/shard_map/while/body/eval_jaxpr/ppermute | solution.py:14
  30.0 5.3 %copy-start.3 = (s32[128,4]{0,1:T(4,128)S(1)}, s32[128,4]{0,1:T(4,128)}, u32[]{:S(2)}) copy-start(s32[128,4]{0,1:T(4,128)} %param.18) | copy-start | bytes 6148
  35.3 20.5 %copy-start.2 = (bf16[128,2880]{0,1:T(8,128)(2,1)S(1)}, bf16[128,2880]{0,1:T(8,128)(2,1)}, u32[]{:S(2)}) copy-start(bf16[128,2880]{0,1:T(8,128)(2,1)} %param.12) | copy-start | bytes 2211844
  35.3 121.2 %all-gather.3.cloned.1.call-start = ((), (), s32[]{:S(2)}) async-start(), calls=%async_computation.3 | async-start | bytes 5308416 | tf_op jit(solution)/shard_map/all_gather | solution.py:143
  56.8 0.7 copy-start.1
  175.3 4.9 %copy-start = (f32[2880,576]{0,1:T(8,128)S(1)}, f32[2880,576]{0,1:T(8,128)}, u32[]{:S(2)}) copy-start(f32[2880,576]{0,1:T(8,128)} %reshape.128) | copy-start | bytes 19906564
  175.3 4.9 %copy-start.4 = (f32[2880]{0:T(1024)S(1)}, f32[2880]{0:T(1024)}, u32[]{:S(2)}) copy-start(f32[2880]{0:T(1024)} %param.17) | copy-start | bytes 34564
Sparse Core Ops, SparseCore 0:
  35.4 20.2 reduce-scatter.1
  109.2 47.2 all-gather.2
where the time goes:
time: 198 us; the launch traced here: 197 us
  waiting for transfers between devices  58 us (29%)
  blocking collectives  50.8 us (26%)
  local copies, waits for them, and re-layouts  37.9 us (19%)
  matrix products  16.6 us (8%)
  between operations  15.6 us (8%)
  other arithmetic  9.75 us (5%)
  starting transfers between devices  8.24 us (4%)
    all_to_all x1, blocking collectives, body(): lax.all_to_all(outgoing.reshape(experts_all, capacity, column_width), 'ct...  46.6 us
    all_gather x1, waiting for transfers between devices, body(): lax.all_gather(arrived_rows, 'head', axis=1, tiled=True).astype(jnp.float32)  38.5 us
    reduce_scatter x1, waiting for transfers between devices, body(): lax.psum_scatter(partial_value.astype(jnp.bfloat16), 'head', scatter_dime...  19.5 us
    convert_element_type x2, local copies, waits for them, and re-layouts, body(): lax.all_gather(arrived_rows, 'head', axis=1, tiled=True).astype(jnp.float32)  18.8 us
    unnamed x15, local copies, waits for them, and re-layouts  13.9 us
    dot_general x1, matrix products, body(): gate_up = jnp.dot(scaled, local_weight, preferred_element_type=jnp.float32)  8.21 us
    ppermute x2, starting transfers between devices, shifted(): return lax.ppermute(value, axis, pairs)  8.17 us
    dot_general x1, matrix products, body(): jnp.dot(attended, out_weight, preferred_element_type=jnp.float32)  5.25 us
  transfers between devices with their start and end apart: 4, of which 2 were waited for; matrix products, arithmetic and copies ran while one was open for 9% of the time, Pallas kernels for 0%

commit v1 on v0

--- a/solution.py
+++ b/solution.py
@@ -6,6 +6,29 @@
 D = 2880
 HD = 64
 TOP = 4
+
+
+def laid_out(tiles, dim):
+    tiles = jnp.moveaxis(tiles, 0, dim)
+    dims = tiles.shape
+    return tiles.reshape(*dims[:dim], dims[dim] * dims[dim + 1], *dims[dim + 2 :])
+
+
+def grow_blocks(value, axis):
+    length, index = (lax.axis_size(axis), lax.axis_index(axis))
+    pieces, bit = (value[None], 1)
+    while bit < length:
+        received = lax.ppermute(pieces, axis, [(i, i ^ bit) for i in range(length)])
+        low = index & bit == 0
+        pieces = jnp.concatenate(
+            [jnp.where(low, pieces, received), jnp.where(low, received, pieces)]
+        )
+        bit *= 2
+    return pieces
+
+
+def doubled_up(shard, axis, dim):
+    return laid_out(grow_blocks(shard, axis), dim)
 
 
 def shifted(value, axis, by):
@@ -140,7 +163,7 @@
     )
     arrived_rows = arrived.reshape(-1, column_width)
     slot_total = arrived_rows.shape[0]
-    widened = lax.all_gather(arrived_rows, "head", axis=1, tiled=True).astype(jnp.float32)
+    widened = doubled_up(arrived_rows, "head", 1).astype(jnp.float32)
     scaled = (widened * norm_gain[None, :]).astype(jnp.bfloat16)
     gate_up = jnp.dot(scaled, local_weight, preferred_element_type=jnp.float32)
     squares = jnp.sum(widened * widened, axis=1)

time: 198 us -> 178 us (0.90)
  local copies, waits for them, and re-layouts: 37.9 us -> 27.8 us
  waiting for transfers between devices: 58 us -> 49 us
    all_gather x1 -> x0, waiting for transfers between devices: 38.5 us -> none  [body(): lax.all_gather(arrived_rows, 'head', axis=1, tiled=True).astype(jnp.float32)]
    ppermute x0 -> x1, waiting for transfers between devices: none -> 29.3 us  [grow_blocks(): received = lax.ppermute(pieces, axis, [(i, i ^ bit) for i in range(length)])]
    convert_element_type x2, local copies, waits for them, and re-layouts: 18.8 us -> 7.89 us  [body(): scaled = (widened * norm_gain[None, :]).astype(jnp.bfloat16)]
    reduce_sum x1, other arithmetic: 3.61 us -> 1.5 us  [body(): squares = jnp.sum(widened * widened, axis=1)]
    unnamed x15 -> x11, local copies, waits for them, and re-layouts: 13.9 us -> 12.2 us
  transfers between devices with their start and end apart: 4 -> 4, of which waited for: 2 -> 2; matrix products, arithmetic and copies ran while one was open for 9% -> 10% of each run, Pallas kernels for 0% -> 0%
where the time goes in v1:
time: 178 us; the launch traced here: 177 us
  blocking collectives  50.6 us (28%)
  waiting for transfers between devices  49 us (28%)
  local copies, waits for them, and re-layouts  27.8 us (16%)
  matrix products  17.5 us (10%)
  between operations  15.6 us (9%)
  starting transfers between devices  8.77 us (5%)
  other arithmetic  7.86 us (4%)
    all_to_all x1, blocking collectives, body(): lax.all_to_all(outgoing.reshape(experts_all, capacity, column_width), 'ct...  46.5 us
    ppermute x1, waiting for transfers between devices, grow_blocks(): received = lax.ppermute(pieces, axis, [(i, i ^ bit) for i in range(length)])  29.3 us
    reduce_scatter x1, waiting for transfers between devices, body(): lax.psum_scatter(partial_value.astype(jnp.bfloat16), 'head', scatter_dime...  19.6 us
    unnamed x11, local copies, waits for them, and re-layouts  12.2 us
    dot_general x1, matrix products, body(): gate_up = jnp.dot(scaled, local_weight, preferred_element_type=jnp.float32)  9.15 us
    ppermute x2, starting transfers between devices, shifted(): return lax.ppermute(value, axis, pairs)  8.17 us
    convert_element_type x2, local copies, waits for them, and re-layouts, body(): scaled = (widened * norm_gain[None, :]).astype(jnp.bfloat16)  7.89 us
    dot_general x1, matrix products, body(): jnp.dot(attended, out_weight, preferred_element_type=jnp.float32)  5.24 us
  transfers between devices with their start and end apart: 4, of which 2 were waited for; matrix products, arithmetic and copies ran while one was open for 10% of the time, Pallas kernels for 0%

profile of v1, /device:TPU:0, one launch (start us, length us, event | category | flops | bytes accessed | tf_op | source)
XLA Modules:
  0.0 177.1 jit_solution(11184137020403830586)
XLA Ops:
  7.2 0.0 reduce-scatter.2.cloned.1.call-start
  7.2 0.9 copy.28
  8.1 2.2 %all_gather.7 = bf16[256,128]{0,1:T(8,128)(2,1)} all-gather(bf16[128,128]{0,1:T(8,128)(2,1)S(1)} %copy.28), channel_id=1, replica_groups=mesh['ctx'=8,'grp'=2,'head'=2] {'grp'}, dimensions={0}, use_global_device_ids=true | all-gather | bytes 98304 | tf_op jit(solution)/shard_map/all_gather | solution.py:95
  10.2 4.7 %collective-permute-start.1 = (bf16[256,128]{0,1:T(8,128)(2,1)}, bf16[256,128]{0,1:T(8,128)(2,1)S(1)}, u32[]{:S(2)}, u32[]{:S(2)}) collective-permute-start(bf16[256,128]{0,1:T(8,128)(2,1)} %all_gather.7), channel_id=1, source_target_pairs={{0,4},{4,8},{8,12},{12,16},{16,20},{20,24},{24,28},{1,5},{5,9},{9,... | collective-permute-start | bytes 196616 | tf_op jit(solution)/shard_map/while/body/eval_jaxpr/ppermute | solution.py:37
  15.0 0.9 copy.26
  15.9 2.0 %all_gather.6 = bf16[256,128]{0,1:T(8,128)(2,1)} all-gather(bf16[128,128]{0,1:T(8,128)(2,1)S(1)} %copy.26), channel_id=1, replica_groups=mesh['ctx'=8,'grp'=2,'head'=2] {'grp'}, dimensions={0}, use_global_device_ids=true | all-gather | bytes 98304 | tf_op jit(solution)/shard_map/all_gather | solution.py:94
  17.9 3.4 %collective-permute-start = (bf16[256,128]{0,1:T(8,128)(2,1)}, bf16[256,128]{0,1:T(8,128)(2,1)S(1)}, u32[]{:S(2)}, u32[]{:S(2)}) collective-permute-start(bf16[256,128]{0,1:T(8,128)(2,1)} %all_gather.6), channel_id=1, source_target_pairs={{0,4},{4,8},{8,12},{12,16},{16,20},{20,24},{24,28},{1,5},{5,9},{9,... | collective-permute-start | bytes 196616 | tf_op jit(solution)/shard_map/while/body/eval_jaxpr/ppermute | solution.py:37
  21.4 0.8 fusion.46
  23.5 1.1 copy.27
  24.6 5.3 %conditional.2 = (f32[2,8,128]{2,1,0:T(8,128)}, f32[2,8,128]{2,1,0:T(8,128)S(1)}, f32[2,8,128,64]{2,3,1,0:T(8,128)S(1)}) conditional(s32[]{:T(128)} %convert_element_type.74, () %tuple.30, (pred[128,256]{0,1:T(8,128)(4,1)S(1)}, bf16[256,128]{0,1:T(8,128)(2,1)}, bf16[128,2,8,64]{0,3,2,1:T(8,128)(2,1)S(1)}, bf16[256,128]{0,1:T(8,128)(2,1)}) %tuple.54), branch_computations={%region_2.3_spmd, %region_3.6_spmd} | conditional | flops 141172736 | bytes 7397400 | solution.py:68
  24.6 1.3 fusion
  26.0 0.6 exponential_multiply_fusion
  26.6 1.2 fusion.2
  27.8 1.4 convolution_add_fusion
  29.2 0.7 fusion.11
  29.9 0.0 collective-permute-done.1
  29.9 0.0 collective-permute-done
  30.0 0.1 divide_convert_fusion
  30.0 0.0 copy-start.2
  30.0 5.2 %convolution_convert_fusion = bf16[128,2880]{0,1:T(8,128)(2,1)} fusion(bf16[1024,2880]{0,1:T(8,128)(2,1)} %param.16, bf16[128,1024]{0,1:T(8,128)(2,1)S(1)} %bitcast.78), kind=kOutput, calls=%fused_computation.36 | convolution fusion | flops 755343360 | bytes 6897664 | tf_op jit(solution)/shard_map/dot_general | solution.py:131
  35.3 0.0 copy-start.1
  35.3 0.0 reduce-scatter.2.cloned.1.call-update
  35.3 0.0 copy-done.2
  35.3 0.1 copy.30
  35.4 0.1 copy.29
  35.6 0.1 mul.114
  35.7 0.1 eq.19
  35.8 0.3 fusion.29
  36.2 19.6 %reduce-scatter.2.cloned.1.call-done = bf16[128,1440]{0,1:T(8,128)(2,1)} async-done(((bf16[128,2880]{0,1:T(8,128)(2,1)}), bf16[128,1440]{0,1:T(8,128)(2,1)}) %reduce-scatter.2.cloned.1.call-update) | async-done | bytes 368656 | tf_op jit(solution)/shard_map/reduce_scatter | solution.py:145
  55.8 0.0 copy-done.1
  55.8 1.1 add_convert_fusion
  56.9 0.0 copy-start
  56.9 0.7 copy-done
  57.6 0.2 copy.31
  57.8 0.4 broadcast_in_dim.79
  58.2 1.7 reshape.124
  59.9 4.3 %scatter_custom_fusion = bf16[576,1440]{1,0:T(8,128)(2,1)S(1)} fusion(s32[512]{0:T(512)S(1)} %bitcast.81, bf16[512,1440]{1,0:T(8,128)(2,1)} %reshape.124, bf16[]{:T(256)} %constant.51.clone.1), kind=kCustom, calls=%fused_computation.50 | custom fusion | bytes 1659392 | tf_op jit(solution)/shard_map/scatter | solution.py:155
  64.2 46.5 %all_to_all.12 = bf16[8,72,1440]{2,1,0:T(8,128)(2,1)S(1)} all-to-all(bf16[8,72,1440]{2,1,0:T(8,128)(2,1)S(1)} %bitcast.75), channel_id=1, replica_groups=mesh['ctx'=8,'grp'=2,'head'=2] {'ctx'}, dimensions={0} | all-to-all | bytes 3317760 | tf_op jit(solution)/shard_map/all_to_all | solution.py:157
  110.7 0.6 collective-permute-start.2
  111.2 0.8 mul.116
  112.0 8.5 %copy.39 = bf16[360,8,2,768]{3,1,2,0:T(8,128)(2,1)} copy(bf16[360,8,2,768]{3,2,1,0:T(2,128)(2,1)} %bitcast.71) | data formatting | bytes 17694720
  120.5 29.3 %collective-permute-done.2 = bf16[1,576,1440]{2,1,0:T(8,128)(2,1)S(1)} collective-permute-done((bf16[1,576,1440]{2,1,0:T(8,128)(2,1)S(1)}, bf16[1,576,1440]{2,1,0:T(8,128)(2,1)S(1)}, u32[]{:S(2)}, u32[]{:S(2)}) %collective-permute-start.2) | collective-permute-done | bytes 1658912 | tf_op jit(solution)/shard_map/ppermute | solution.py:21
  149.8 0.2 broadcast_select_fusion.1
  150.1 1.5 fusion.24
  151.6 3.6 %copy.32 = bf16[576,2,1440]{2,1,0:T(2,128)(2,1)S(1)} copy(bf16[576,2,1440]{2,0,1:T(8,128)(2,1)S(1)} %get-tuple-element.110) | data formatting | bytes 6635520 | tf_op jit(solution)/shard_map/convert_element_type | solution.py:167
  155.3 4.2 %convert_element_type.88 = bf16[576,2880]{1,0:T(8,128)(2,1)} reshape(bf16[576,2,1440]{2,1,0:T(2,128)(2,1)S(1)} %copy.32) | data formatting | bytes 6635520 | tf_op jit(solution)/shard_map/convert_element_type | solution.py:167
  159.5 9.2 %fusion.48 = f32[576,1536]{1,0:T(8,128)S(1)} fusion(bf16[576,2880]{1,0:T(8,128)(2,1)} %convert_element_type.88, bf16[2880,1536]{1,0:T(8,128)(2,1)} %bitcast.72), kind=kOutput, calls=%fused_computation.80 | convolution fusion | flops 5096079360 | bytes 15704064 | tf_op jit(solution)/shard_map/dot_general | solution.py:168
  168.7 1.6 fusion.33
  (9 shorter events, 0.1 us)
Async XLA Ops:
  7.2 48.6 %reduce-scatter.2.cloned.1.call-start = ((), (), s32[]{:S(2)}) async-start(), calls=%async_computation.2 | async-start | bytes 1105920 | tf_op jit(solution)/shard_map/reduce_scatter | solution.py:145
  10.2 19.7 %collective-permute-start.1 = (bf16[256,128]{0,1:T(8,128)(2,1)}, bf16[256,128]{0,1:T(8,128)(2,1)S(1)}, u32[]{:S(2)}, u32[]{:S(2)}) collective-permute-start(bf16[256,128]{0,1:T(8,128)(2,1)} %all_gather.7), channel_id=1, source_target_pairs={{0,4},{4,8},{8,12},{12,16},{16,20},{20,24},{24,28},{1,5},{5,9},{9,... | collective-permute-start | bytes 196616 | tf_op jit(solution)/shard_map/while/body/eval_jaxpr/ppermute | solution.py:37
  17.9 12.1 %collective-permute-start = (bf16[256,128]{0,1:T(8,128)(2,1)}, bf16[256,128]{0,1:T(8,128)(2,1)S(1)}, u32[]{:S(2)}, u32[]{:S(2)}) collective-permute-start(bf16[256,128]{0,1:T(8,128)(2,1)} %all_gather.6), channel_id=1, source_target_pairs={{0,4},{4,8},{8,12},{12,16},{16,20},{20,24},{24,28},{1,5},{5,9},{9,... | collective-permute-start | bytes 196616 | tf_op jit(solution)/shard_map/while/body/eval_jaxpr/ppermute | solution.py:37
  30.0 5.3 %copy-start.2 = (s32[128,4]{0,1:T(4,128)S(1)}, s32[128,4]{0,1:T(4,128)}, u32[]{:S(2)}) copy-start(s32[128,4]{0,1:T(4,128)} %param.18) | copy-start | bytes 6148
  35.3 20.5 %copy-start.1 = (bf16[128,2880]{0,1:T(8,128)(2,1)S(1)}, bf16[128,2880]{0,1:T(8,128)(2,1)}, u32[]{:S(2)}) copy-start(bf16[128,2880]{0,1:T(8,128)(2,1)} %param.12) | copy-start | bytes 2211844
  56.9 0.7 copy-start
  110.7 39.2 %collective-permute-start.2 = (bf16[1,576,1440]{2,1,0:T(8,128)(2,1)S(1)}, bf16[1,576,1440]{2,1,0:T(8,128)(2,1)S(1)}, u32[]{:S(2)}, u32[]{:S(2)}) collective-permute-start(bf16[1,576,1440]{2,1,0:T(8,128)(2,1)S(1)} %bitcast.73), channel_id=1, source_target_pairs={{0,1},{1,0},{2,3},{3,2},{4,5},{5,4},{6,7},{7,6},{8,9},{9,8},{10,11... | collective-permute-start | bytes 4976648 | tf_op jit(solution)/shard_map/ppermute | solution.py:21
Sparse Core Ops, SparseCore 0:
  35.4 20.2 reduce-scatter.1
